TPU v7x, 256 devices: a whole 4x4x8 slice. The times are simulated.
256 devices in a mesh: ctx: 16 (over z, core), row: 4 (over y), col: 4 (over x).
Axes of the slice: x: 4, y: 4, z: 8, core: 2. Of those that a mesh axis runs over, the one named last changes fastest.
Arguments:
- output_grad: bfloat16 [8192, 8192], P('ctx', ('row', 'col')), may hold values from -6 to 6
- conv_out: bfloat16 [8192, 8192], P('ctx', ('row', 'col')), may hold values from -9 to 9
- input_mix: bfloat16 [8192, 4, 256], P('ctx'), may hold values from -0.15625 to 0.15625
- output_mix: bfloat16 [8192, 4, 256], P('ctx'), may hold values from -1 to 1
- step_size: float32 [128, 8192], P(('row', 'col'), 'ctx'), may hold values from 0.5 to 2
- log_decay: float32 [128, 8192], P(('row', 'col'), 'ctx'), may hold values from -2.1 to 0, as said below
- skip_gain: float32 [128], P(('row', 'col')), may hold values from 0.5 to 2
- conv_weight: float32 [4, 8192], P(None, ('row', 'col')), may hold values from -3 to 3
- later_grad: float32 [128, 64, 256], P(('row', 'col')), may hold values from -32 to 32
- proj_weight: bfloat16 [8192, 8192], P('col', 'row'), may hold values from -0.0625 to 0.0625
Outputs:
- hidden_grad: bfloat16 [8192, 8192], P('ctx', ('col', 'row'))
- x_grad: bfloat16 [8192, 8192], P('ctx', ('row', 'col'))
- state_grad: float32 [16, 128, 64, 256], P('ctx', ('row', 'col'))
Inputs may be any that keep to these rules, and one draw needn't show every extreme that they name: `log_decay`: the forward pass's log decay of each head at each token.
All inputs are finite; a program needn't handle non-finite values.
Results may differ from a plain program's by a relative error of at most 0.022.
Values may be sent and summed in bfloat16 or wider, within the bound.
No kernel may reach another device: no remote copies, remote signals or barrier semaphores. Data moves between devices by JAX's collectives and lax.ppermute only.
A program may use at most 128 MiB of HBM per device.

v0:
```python
import jax
import jax.numpy as jnp
from jax import lax
from jax.sharding import PartitionSpec as P

HD = 64
HPG = 32
KW = 4


def from_behind(value, axis, steps):
    count = lax.axis_size(axis)
    first, last = (max(0, -steps), min(count, count - steps))
    return lax.ppermute(value, axis, [(source, source + steps) for source in range(first, last)])


def on_device(
    output_grad,
    conv_out,
    input_mix,
    output_mix,
    step_size,
    log_decay,
    skip_gain,
    conv_weight,
    later_grad,
    proj_weight,
):
    tokens_dev = output_grad.shape[0]
    heads_dev = step_size.shape[0]
    head_block = lax.axis_index("row") * lax.axis_size("col") + lax.axis_index("col")
    group = head_block * heads_dev // HPG
    write_rows = lax.dynamic_index_in_dim(input_mix, group, 1, keepdims=False)
    read_rows = lax.dynamic_index_in_dim(output_mix, group, 1, keepdims=False)
    cumulative = jnp.cumsum(log_decay, axis=1)
    block_end = cumulative[:, -1]
    decays = jnp.exp(block_end)
    per_head = output_grad.reshape(tokens_dev, heads_dev, HD)
    weighted = (jnp.exp(cumulative).T[:, :, None] * per_head.astype(jnp.float32)).astype(
        jnp.bfloat16
    )
    block_sum = jnp.einsum("shd,sn->hdn", weighted, read_rows, preferred_element_type=jnp.float32)
    is_last = lax.axis_index("ctx") == lax.axis_size("ctx") - 1

    def chain_turn(turn_index, estimate):
        passed = from_behind(
            (block_sum + decays[:, None, None] * estimate).astype(jnp.bfloat16), "ctx", -1
        ).astype(jnp.float32)
        return jnp.where(is_last, later_grad, passed)

    carried = lax.fori_loop(
        0,
        lax.axis_size("ctx") - 1,
        chain_turn,
        jnp.where(is_last, later_grad, jnp.zeros_like(later_grad)),
    )
    state_start = block_sum + decays[:, None, None] * carried
    scores = jnp.dot(write_rows, read_rows.T, preferred_element_type=jnp.float32)
    positions = jnp.arange(tokens_dev)
    causal = positions[None, :] >= positions[:, None]
    offsets = cumulative[:, None, :] - cumulative[:, :, None]
    mixing = (jnp.exp(jnp.where(causal[None], offsets, -jnp.inf)) * scores[None]).astype(
        jnp.bfloat16
    )
    intra = jnp.einsum("hts,shd->thd", mixing, per_head, preferred_element_type=jnp.float32)
    inter = jnp.einsum(
        "hdn,tn->thd", carried, write_rows.astype(jnp.float32), precision=lax.Precision.HIGHEST
    )
    inter = inter * jnp.exp(block_end[:, None] - cumulative).T[:, :, None]
    input_grad = step_size.T[:, :, None] * (intra + inter) + skip_gain[
        None, :, None
    ] * per_head.astype(jnp.float32)
    flat_grad = input_grad.reshape(tokens_dev, heads_dev * HD)
    activated = conv_out.astype(jnp.float32)
    sigma = jax.nn.sigmoid(activated)
    pre_grad = (flat_grad * sigma * (1.0 + activated * (1.0 - sigma))).astype(jnp.bfloat16)
    rim_rows = from_behind(pre_grad[: KW - 1], "ctx", -1)
    extended = jnp.concatenate([pre_grad, rim_rows], axis=0).astype(jnp.float32)
    accum = jnp.zeros(pre_grad.shape, jnp.float32)
    for tap in range(KW):
        accum = accum + conv_weight[tap][None, :] * extended[tap : tap + tokens_dev]
    x_grad = accum.astype(jnp.bfloat16)
    partial_grad = lax.dot_general(
        lax.all_gather(x_grad, "col", axis=1, tiled=True),
        proj_weight,
        (((1,), (1,)), ((), ())),
        preferred_element_type=jnp.float32,
    )
    hidden_grad = lax.psum_scatter(
        partial_grad.astype(jnp.bfloat16), "row", scatter_dimension=1, tiled=True
    )
    return (hidden_grad, x_grad, state_start[None])


def solution(mesh):
    return jax.shard_map(
        on_device,
        mesh=mesh,
        in_specs=(
            P("ctx", ("row", "col")),
            P("ctx", ("row", "col")),
            P("ctx", None, None),
            P("ctx", None, None),
            P(("row", "col"), "ctx"),
            P(("row", "col"), "ctx"),
            P(("row", "col")),
            P(None, ("row", "col")),
            P(("row", "col"), None, None),
            P("col", "row"),
        ),
        out_specs=(
            P("ctx", ("col", "row")),
            P("ctx", ("row", "col")),
            P("ctx", ("row", "col"), None, None),
        ),
        check_vma=False,
    )
```

profile of v0, /device:TPU:1, one launch (start us, length us, event | category | flops | bytes accessed | tf_op | source)
XLA Modules:
  0.0 251.9 jit_solution(11634387616972478772)
XLA Ops:
  7.2 2.3 reduce-window.6
  9.8 0.2 slice_reduce_fusion.1
  10.1 1.3 copy.26
  11.5 2.6 %constant_dynamic-slice_fusion = (bf16[512,1,256]{2,1,0:T(2,128)(2,1)S(1)}, bf16[512,1,256]{2,1,0:T(2,128)(2,1)S(1)}) fusion(bf16[512,4,256]{2,1,0:T(4,128)(2,1)} %param.15, s32[]{:T(128)S(6)} %select_n.30, bf16[512,4,256]{2,1,0:T(4,128)(2,1)} %param.14), kind=kLoop, calls=%fused_computation.48 | loop fusion | bytes 1048580 | tf_op jit(solution)/shard_map/jit(dynamic_index_in_dim)/dynamic_slice | solution.py:34
  14.1 0.3 fusion.17
  14.5 1.3 fusion.20
  15.8 4.3 %fusion.2 = f32[512,8,64]{0,2,1:T(8,128)} fusion(bf16[512,8,64]{0,2,1:T(8,128)(2,1)S(1)} %bitcast.41, f32[512,512]{1,0:T(8,128)} %fusion.20, f32[8,512]{1,0:T(8,128)S(1)} %get-tuple-element.49, pred[512,512]{1,0:T(8,128)(4,1)S(1)} %iota_compare_fusion), kind=kOutput, calls=%fused_computation.6 | convolution fusion | flops 276824064 | bytes 2899968 | tf_op jit(solution)/shard_map/hts,shd->thd/dot_general | solution.py:65
  20.1 119.6 %while.10 = (s32[]{:T(128)}, f32[8,64,256]{2,1,0:T(8,128)S(1)}, pred[]{:T(512)}, f32[8]{0:T(128)S(1)}, f32[8,64,256]{2,1,0:T(8,128)S(1)}, /*index=5*/f32[8,64,256]{2,1,0:T(8,128)S(1)}, s32[]{:T(128)}) while((s32[]{:T(128)}, f32[8,64,256]{2,1,0:T(8,128)S(1)}, pred[]{:T(512)}, f32[8]{0:T(128)S(1)}, f32[8,64,256]{2,1,0:T(8,128)S(1)}, ...), condition=%wide.region_3.4_spmd, body=%wide.region_2.3_spmd.sunk | while | flops 655362 | bytes 3670166 | solution.py:51
  20.2 5.2 %collective-permute-start = (bf16[8,64,256]{2,1,0:T(8,128)(2,1)S(1)}, bf16[8,64,256]{2,1,0:T(8,128)(2,1)S(1)}, u32[]{:S(2)}, u32[]{:S(2)}) collective-permute-start(bf16[8,64,256]{2,1,0:T(8,128)(2,1)S(1)} %add_convert_fusion.2), channel_id=1, source_target_pairs={{16,0},{32,16},{48,32},{64,48},{80,64},{96,80},{112,96},{128,112},... | collective-permute-start | bytes 786440 | tf_op jit(solution)/shard_map/while/body/eval_jaxpr/ppermute | solution.py:14
  25.4 3.8 %collective-permute-done = bf16[8,64,256]{2,1,0:T(8,128)(2,1)S(1)} collective-permute-done((bf16[8,64,256]{2,1,0:T(8,128)(2,1)S(1)}, bf16[8,64,256]{2,1,0:T(8,128)(2,1)S(1)}, u32[]{:S(2)}, u32[]{:S(2)}) %collective-permute-start) | collective-permute-done | bytes 262176 | tf_op jit(solution)/shard_map/while/body/eval_jaxpr/ppermute | solution.py:14
  29.4 1.9 collective-permute-start
  31.3 5.8 %collective-permute-done = bf16[8,64,256]{2,1,0:T(8,128)(2,1)S(1)} collective-permute-done((bf16[8,64,256]{2,1,0:T(8,128)(2,1)S(1)}, bf16[8,64,256]{2,1,0:T(8,128)(2,1)S(1)}, u32[]{:S(2)}, u32[]{:S(2)}) %collective-permute-start) | collective-permute-done | bytes 262176 | tf_op jit(solution)/shard_map/while/body/eval_jaxpr/ppermute | solution.py:14
  37.3 1.9 collective-permute-start
  39.2 5.8 %collective-permute-done = bf16[8,64,256]{2,1,0:T(8,128)(2,1)S(1)} collective-permute-done((bf16[8,64,256]{2,1,0:T(8,128)(2,1)S(1)}, bf16[8,64,256]{2,1,0:T(8,128)(2,1)S(1)}, u32[]{:S(2)}, u32[]{:S(2)}) %collective-permute-start) | collective-permute-done | bytes 262176 | tf_op jit(solution)/shard_map/while/body/eval_jaxpr/ppermute | solution.py:14
  45.2 1.9 collective-permute-start
  47.1 5.8 %collective-permute-done = bf16[8,64,256]{2,1,0:T(8,128)(2,1)S(1)} collective-permute-done((bf16[8,64,256]{2,1,0:T(8,128)(2,1)S(1)}, bf16[8,64,256]{2,1,0:T(8,128)(2,1)S(1)}, u32[]{:S(2)}, u32[]{:S(2)}) %collective-permute-start) | collective-permute-done | bytes 262176 | tf_op jit(solution)/shard_map/while/body/eval_jaxpr/ppermute | solution.py:14
  53.1 1.9 collective-permute-start
  55.0 5.8 %collective-permute-done = bf16[8,64,256]{2,1,0:T(8,128)(2,1)S(1)} collective-permute-done((bf16[8,64,256]{2,1,0:T(8,128)(2,1)S(1)}, bf16[8,64,256]{2,1,0:T(8,128)(2,1)S(1)}, u32[]{:S(2)}, u32[]{:S(2)}) %collective-permute-start) | collective-permute-done | bytes 262176 | tf_op jit(solution)/shard_map/while/body/eval_jaxpr/ppermute | solution.py:14
  60.9 1.9 collective-permute-start
  62.9 5.8 %collective-permute-done = bf16[8,64,256]{2,1,0:T(8,128)(2,1)S(1)} collective-permute-done((bf16[8,64,256]{2,1,0:T(8,128)(2,1)S(1)}, bf16[8,64,256]{2,1,0:T(8,128)(2,1)S(1)}, u32[]{:S(2)}, u32[]{:S(2)}) %collective-permute-start) | collective-permute-done | bytes 262176 | tf_op jit(solution)/shard_map/while/body/eval_jaxpr/ppermute | solution.py:14
  68.8 1.9 collective-permute-start
  70.8 5.8 %collective-permute-done = bf16[8,64,256]{2,1,0:T(8,128)(2,1)S(1)} collective-permute-done((bf16[8,64,256]{2,1,0:T(8,128)(2,1)S(1)}, bf16[8,64,256]{2,1,0:T(8,128)(2,1)S(1)}, u32[]{:S(2)}, u32[]{:S(2)}) %collective-permute-start) | collective-permute-done | bytes 262176 | tf_op jit(solution)/shard_map/while/body/eval_jaxpr/ppermute | solution.py:14
  76.7 1.9 collective-permute-start
  78.6 5.8 %collective-permute-done = bf16[8,64,256]{2,1,0:T(8,128)(2,1)S(1)} collective-permute-done((bf16[8,64,256]{2,1,0:T(8,128)(2,1)S(1)}, bf16[8,64,256]{2,1,0:T(8,128)(2,1)S(1)}, u32[]{:S(2)}, u32[]{:S(2)}) %collective-permute-start) | collective-permute-done | bytes 262176 | tf_op jit(solution)/shard_map/while/body/eval_jaxpr/ppermute | solution.py:14
  84.6 1.9 collective-permute-start
  86.5 5.8 %collective-permute-done = bf16[8,64,256]{2,1,0:T(8,128)(2,1)S(1)} collective-permute-done((bf16[8,64,256]{2,1,0:T(8,128)(2,1)S(1)}, bf16[8,64,256]{2,1,0:T(8,128)(2,1)S(1)}, u32[]{:S(2)}, u32[]{:S(2)}) %collective-permute-start) | collective-permute-done | bytes 262176 | tf_op jit(solution)/shard_map/while/body/eval_jaxpr/ppermute | solution.py:14
  92.5 1.9 collective-permute-start
  94.4 5.8 %collective-permute-done = bf16[8,64,256]{2,1,0:T(8,128)(2,1)S(1)} collective-permute-done((bf16[8,64,256]{2,1,0:T(8,128)(2,1)S(1)}, bf16[8,64,256]{2,1,0:T(8,128)(2,1)S(1)}, u32[]{:S(2)}, u32[]{:S(2)}) %collective-permute-start) | collective-permute-done | bytes 262176 | tf_op jit(solution)/shard_map/while/body/eval_jaxpr/ppermute | solution.py:14
  100.4 1.9 collective-permute-start
  102.3 5.8 %collective-permute-done = bf16[8,64,256]{2,1,0:T(8,128)(2,1)S(1)} collective-permute-done((bf16[8,64,256]{2,1,0:T(8,128)(2,1)S(1)}, bf16[8,64,256]{2,1,0:T(8,128)(2,1)S(1)}, u32[]{:S(2)}, u32[]{:S(2)}) %collective-permute-start) | collective-permute-done | bytes 262176 | tf_op jit(solution)/shard_map/while/body/eval_jaxpr/ppermute | solution.py:14
  108.3 1.9 collective-permute-start
  110.2 5.8 %collective-permute-done = bf16[8,64,256]{2,1,0:T(8,128)(2,1)S(1)} collective-permute-done((bf16[8,64,256]{2,1,0:T(8,128)(2,1)S(1)}, bf16[8,64,256]{2,1,0:T(8,128)(2,1)S(1)}, u32[]{:S(2)}, u32[]{:S(2)}) %collective-permute-start) | collective-permute-done | bytes 262176 | tf_op jit(solution)/shard_map/while/body/eval_jaxpr/ppermute | solution.py:14
  116.2 1.9 collective-permute-start
  118.1 5.8 %collective-permute-done = bf16[8,64,256]{2,1,0:T(8,128)(2,1)S(1)} collective-permute-done((bf16[8,64,256]{2,1,0:T(8,128)(2,1)S(1)}, bf16[8,64,256]{2,1,0:T(8,128)(2,1)S(1)}, u32[]{:S(2)}, u32[]{:S(2)}) %collective-permute-start) | collective-permute-done | bytes 262176 | tf_op jit(solution)/shard_map/while/body/eval_jaxpr/ppermute | solution.py:14
  124.0 1.9 collective-permute-start
  126.0 5.8 %collective-permute-done = bf16[8,64,256]{2,1,0:T(8,128)(2,1)S(1)} collective-permute-done((bf16[8,64,256]{2,1,0:T(8,128)(2,1)S(1)}, bf16[8,64,256]{2,1,0:T(8,128)(2,1)S(1)}, u32[]{:S(2)}, u32[]{:S(2)}) %collective-permute-start) | collective-permute-done | bytes 262176 | tf_op jit(solution)/shard_map/while/body/eval_jaxpr/ppermute | solution.py:14
  131.9 1.9 collective-permute-start
  133.9 5.8 %collective-permute-done = bf16[8,64,256]{2,1,0:T(8,128)(2,1)S(1)} collective-permute-done((bf16[8,64,256]{2,1,0:T(8,128)(2,1)S(1)}, bf16[8,64,256]{2,1,0:T(8,128)(2,1)S(1)}, u32[]{:S(2)}, u32[]{:S(2)}) %collective-permute-start) | collective-permute-done | bytes 262176 | tf_op jit(solution)/shard_map/while/body/eval_jaxpr/ppermute | solution.py:14
  139.7 2.0 fusion.5
  141.7 0.3 copy.28
  142.0 1.4 fusion.11
  143.5 1.9 collective-permute-start.1
  145.5 3.0 %collective-permute-done.1 = bf16[3,512]{1,0:T(4,128)(2,1)S(1)} collective-permute-done((bf16[3,512]{1,0:T(4,128)(2,1)S(1)}, bf16[3,512]{1,0:T(4,128)(2,1)S(1)}, u32[]{:S(2)}, u32[]{:S(2)}) %collective-permute-start.1) | collective-permute-done | bytes 3104 | tf_op jit(solution)/shard_map/ppermute | solution.py:14
  148.6 1.3 fusion.13
  149.9 52.7 %all-gather.2.cloned.1.call-done = bf16[512,2048]{1,0:T(8,128)(2,1)} async-done(((bf16[512,512]{1,0:T(8,128)(2,1)}), bf16[512,2048]{1,0:T(8,128)(2,1)}) %all-gather.2.cloned.1.call-update) | async-done | bytes 2097168 | tf_op jit(solution)/shard_map/all_gather | solution.py:84
  202.6 9.9 %convolution_convert_fusion = bf16[512,2048]{1,0:T(8,128)(2,1)} fusion(bf16[512,2048]{1,0:T(8,128)(2,1)} %all-gather.2.cloned.1.call-done, bf16[2048,2048]{1,0:T(8,128)(2,1)} %param.21), kind=kOutput, calls=%fused_computation.5 | convolution fusion | flops 4296015872 | bytes 12582912 | tf_op jit(solution)/shard_map/dot_general | solution.py:83
  212.5 0.9 add_bitcast_fusion
  213.4 31.6 %reduce-scatter.2.cloned.1.call-done = bf16[512,512]{1,0:T(8,128)(2,1)} async-done(((bf16[512,2048]{1,0:T(8,128)(2,1)}), bf16[512,512]{1,0:T(8,128)(2,1)}) %reduce-scatter.2.cloned.1.call-update) | async-done | bytes 524304 | tf_op jit(solution)/shard_map/reduce_scatter | solution.py:89
  (54 shorter events, 3.4 us)
Async XLA Ops:
  7.2 8.6 %copy-start = (f32[8,64,256]{2,1,0:T(8,128)S(1)}, f32[8,64,256]{2,1,0:T(8,128)}, u32[]{:S(2)}) copy-start(f32[8,64,256]{2,1,0:T(8,128)} %param.20) | copy-start | bytes 1572868
  7.2 195.4 %all-gather.2.cloned.1.call-start = ((), (), s32[]{:S(2)}) async-start(), calls=%async_computation.1 | async-start | bytes 2621440 | tf_op jit(solution)/shard_map/all_gather | solution.py:84
  20.1 119.6 %copy-start.1 = (f32[8,512]{1,0:T(8,128)S(1)}, f32[8,512]{1,0:T(8,128)}, u32[]{:S(2)}) copy-start(f32[8,512]{1,0:T(8,128)} %param.16) | copy-start | bytes 49156
  20.1 119.6 %copy-start.3 = (f32[8]{0:T(128)S(1)}, f32[8]{0:T(128)}, u32[]{:S(2)}) copy-start(f32[8]{0:T(128)} %param.18) | copy-start | bytes 100
  20.2 9.0 %collective-permute-start = (bf16[8,64,256]{2,1,0:T(8,128)(2,1)S(1)}, bf16[8,64,256]{2,1,0:T(8,128)(2,1)S(1)}, u32[]{:S(2)}, u32[]{:S(2)}) collective-permute-start(bf16[8,64,256]{2,1,0:T(8,128)(2,1)S(1)} %add_convert_fusion.2), channel_id=1, source_target_pairs={{16,0},{32,16},{48,32},{64,48},{80,64},{96,80},{112,96},{128,112},... | collective-permute-start | bytes 786440 | tf_op jit(solution)/shard_map/while/body/eval_jaxpr/ppermute | solution.py:14
  29.4 7.7 %collective-permute-start = (bf16[8,64,256]{2,1,0:T(8,128)(2,1)S(1)}, bf16[8,64,256]{2,1,0:T(8,128)(2,1)S(1)}, u32[]{:S(2)}, u32[]{:S(2)}) collective-permute-start(bf16[8,64,256]{2,1,0:T(8,128)(2,1)S(1)} %add_convert_fusion.2), channel_id=1, source_target_pairs={{16,0},{32,16},{48,32},{64,48},{80,64},{96,80},{112,96},{128,112},... | collective-permute-start | bytes 786440 | tf_op jit(solution)/shard_map/while/body/eval_jaxpr/ppermute | solution.py:14
  37.3 7.7 %collective-permute-start = (bf16[8,64,256]{2,1,0:T(8,128)(2,1)S(1)}, bf16[8,64,256]{2,1,0:T(8,128)(2,1)S(1)}, u32[]{:S(2)}, u32[]{:S(2)}) collective-permute-start(bf16[8,64,256]{2,1,0:T(8,128)(2,1)S(1)} %add_convert_fusion.2), channel_id=1, source_target_pairs={{16,0},{32,16},{48,32},{64,48},{80,64},{96,80},{112,96},{128,112},... | collective-permute-start | bytes 786440 | tf_op jit(solution)/shard_map/while/body/eval_jaxpr/ppermute | solution.py:14
  45.2 7.7 %collective-permute-start = (bf16[8,64,256]{2,1,0:T(8,128)(2,1)S(1)}, bf16[8,64,256]{2,1,0:T(8,128)(2,1)S(1)}, u32[]{:S(2)}, u32[]{:S(2)}) collective-permute-start(bf16[8,64,256]{2,1,0:T(8,128)(2,1)S(1)} %add_convert_fusion.2), channel_id=1, source_target_pairs={{16,0},{32,16},{48,32},{64,48},{80,64},{96,80},{112,96},{128,112},... | collective-permute-start | bytes 786440 | tf_op jit(solution)/shard_map/while/body/eval_jaxpr/ppermute | solution.py:14
  53.1 7.7 %collective-permute-start = (bf16[8,64,256]{2,1,0:T(8,128)(2,1)S(1)}, bf16[8,64,256]{2,1,0:T(8,128)(2,1)S(1)}, u32[]{:S(2)}, u32[]{:S(2)}) collective-permute-start(bf16[8,64,256]{2,1,0:T(8,128)(2,1)S(1)} %add_convert_fusion.2), channel_id=1, source_target_pairs={{16,0},{32,16},{48,32},{64,48},{80,64},{96,80},{112,96},{128,112},... | collective-permute-start | bytes 786440 | tf_op jit(solution)/shard_map/while/body/eval_jaxpr/ppermute | solution.py:14
  60.9 7.7 %collective-permute-start = (bf16[8,64,256]{2,1,0:T(8,128)(2,1)S(1)}, bf16[8,64,256]{2,1,0:T(8,128)(2,1)S(1)}, u32[]{:S(2)}, u32[]{:S(2)}) collective-permute-start(bf16[8,64,256]{2,1,0:T(8,128)(2,1)S(1)} %add_convert_fusion.2), channel_id=1, source_target_pairs={{16,0},{32,16},{48,32},{64,48},{80,64},{96,80},{112,96},{128,112},... | collective-permute-start | bytes 786440 | tf_op jit(solution)/shard_map/while/body/eval_jaxpr/ppermute | solution.py:14
  68.8 7.7 %collective-permute-start = (bf16[8,64,256]{2,1,0:T(8,128)(2,1)S(1)}, bf16[8,64,256]{2,1,0:T(8,128)(2,1)S(1)}, u32[]{:S(2)}, u32[]{:S(2)}) collective-permute-start(bf16[8,64,256]{2,1,0:T(8,128)(2,1)S(1)} %add_convert_fusion.2), channel_id=1, source_target_pairs={{16,0},{32,16},{48,32},{64,48},{80,64},{96,80},{112,96},{128,112},... | collective-permute-start | bytes 786440 | tf_op jit(solution)/shard_map/while/body/eval_jaxpr/ppermute | solution.py:14
  76.7 7.7 %collective-permute-start = (bf16[8,64,256]{2,1,0:T(8,128)(2,1)S(1)}, bf16[8,64,256]{2,1,0:T(8,128)(2,1)S(1)}, u32[]{:S(2)}, u32[]{:S(2)}) collective-permute-start(bf16[8,64,256]{2,1,0:T(8,128)(2,1)S(1)} %add_convert_fusion.2), channel_id=1, source_target_pairs={{16,0},{32,16},{48,32},{64,48},{80,64},{96,80},{112,96},{128,112},... | collective-permute-start | bytes 786440 | tf_op jit(solution)/shard_map/while/body/eval_jaxpr/ppermute | solution.py:14
  84.6 7.7 %collective-permute-start = (bf16[8,64,256]{2,1,0:T(8,128)(2,1)S(1)}, bf16[8,64,256]{2,1,0:T(8,128)(2,1)S(1)}, u32[]{:S(2)}, u32[]{:S(2)}) collective-permute-start(bf16[8,64,256]{2,1,0:T(8,128)(2,1)S(1)} %add_convert_fusion.2), channel_id=1, source_target_pairs={{16,0},{32,16},{48,32},{64,48},{80,64},{96,80},{112,96},{128,112},... | collective-permute-start | bytes 786440 | tf_op jit(solution)/shard_map/while/body/eval_jaxpr/ppermute | solution.py:14
  92.5 7.7 %collective-permute-start = (bf16[8,64,256]{2,1,0:T(8,128)(2,1)S(1)}, bf16[8,64,256]{2,1,0:T(8,128)(2,1)S(1)}, u32[]{:S(2)}, u32[]{:S(2)}) collective-permute-start(bf16[8,64,256]{2,1,0:T(8,128)(2,1)S(1)} %add_convert_fusion.2), channel_id=1, source_target_pairs={{16,0},{32,16},{48,32},{64,48},{80,64},{96,80},{112,96},{128,112},... | collective-permute-start | bytes 786440 | tf_op jit(solution)/shard_map/while/body/eval_jaxpr/ppermute | solution.py:14
  100.4 7.7 %collective-permute-start = (bf16[8,64,256]{2,1,0:T(8,128)(2,1)S(1)}, bf16[8,64,256]{2,1,0:T(8,128)(2,1)S(1)}, u32[]{:S(2)}, u32[]{:S(2)}) collective-permute-start(bf16[8,64,256]{2,1,0:T(8,128)(2,1)S(1)} %add_convert_fusion.2), channel_id=1, source_target_pairs={{16,0},{32,16},{48,32},{64,48},{80,64},{96,80},{112,96},{128,112},... | collective-permute-start | bytes 786440 | tf_op jit(solution)/shard_map/while/body/eval_jaxpr/ppermute | solution.py:14
  108.3 7.7 %collective-permute-start = (bf16[8,64,256]{2,1,0:T(8,128)(2,1)S(1)}, bf16[8,64,256]{2,1,0:T(8,128)(2,1)S(1)}, u32[]{:S(2)}, u32[]{:S(2)}) collective-permute-start(bf16[8,64,256]{2,1,0:T(8,128)(2,1)S(1)} %add_convert_fusion.2), channel_id=1, source_target_pairs={{16,0},{32,16},{48,32},{64,48},{80,64},{96,80},{112,96},{128,112},... | collective-permute-start | bytes 786440 | tf_op jit(solution)/shard_map/while/body/eval_jaxpr/ppermute | solution.py:14
  116.2 7.7 %collective-permute-start = (bf16[8,64,256]{2,1,0:T(8,128)(2,1)S(1)}, bf16[8,64,256]{2,1,0:T(8,128)(2,1)S(1)}, u32[]{:S(2)}, u32[]{:S(2)}) collective-permute-start(bf16[8,64,256]{2,1,0:T(8,128)(2,1)S(1)} %add_convert_fusion.2), channel_id=1, source_target_pairs={{16,0},{32,16},{48,32},{64,48},{80,64},{96,80},{112,96},{128,112},... | collective-permute-start | bytes 786440 | tf_op jit(solution)/shard_map/while/body/eval_jaxpr/ppermute | solution.py:14
  124.0 7.7 %collective-permute-start = (bf16[8,64,256]{2,1,0:T(8,128)(2,1)S(1)}, bf16[8,64,256]{2,1,0:T(8,128)(2,1)S(1)}, u32[]{:S(2)}, u32[]{:S(2)}) collective-permute-start(bf16[8,64,256]{2,1,0:T(8,128)(2,1)S(1)} %add_convert_fusion.2), channel_id=1, source_target_pairs={{16,0},{32,16},{48,32},{64,48},{80,64},{96,80},{112,96},{128,112},... | collective-permute-start | bytes 786440 | tf_op jit(solution)/shard_map/while/body/eval_jaxpr/ppermute | solution.py:14
  131.9 7.7 %collective-permute-start = (bf16[8,64,256]{2,1,0:T(8,128)(2,1)S(1)}, bf16[8,64,256]{2,1,0:T(8,128)(2,1)S(1)}, u32[]{:S(2)}, u32[]{:S(2)}) collective-permute-start(bf16[8,64,256]{2,1,0:T(8,128)(2,1)S(1)} %add_convert_fusion.2), channel_id=1, source_target_pairs={{16,0},{32,16},{48,32},{64,48},{80,64},{96,80},{112,96},{128,112},... | collective-permute-start | bytes 786440 | tf_op jit(solution)/shard_map/while/body/eval_jaxpr/ppermute | solution.py:14
  139.7 5.7 %copy-start.2 = (f32[4,512]{1,0:T(4,128)S(1)}, f32[4,512]{1,0:T(4,128)}, u32[]{:S(2)}) copy-start(f32[4,512]{1,0:T(4,128)} %param.19) | copy-start | bytes 24580
  143.5 4.9 %collective-permute-start.1 = (bf16[3,512]{1,0:T(4,128)(2,1)S(1)}, bf16[3,512]{1,0:T(4,128)(2,1)S(1)}, u32[]{:S(2)}, u32[]{:S(2)}) collective-permute-start(bf16[3,512]{1,0:T(4,128)(2,1)S(1)} %slice.50), channel_id=1, source_target_pairs={{16,0},{32,16},{48,32},{64,48},{80,64},{96,80},{112,96},{128,112},... | collective-permute-start | bytes 9224 | tf_op jit(solution)/shard_map/ppermute | solution.py:14
  149.8 95.2 %reduce-scatter.2.cloned.1.call-start = ((), (), s32[]{:S(2)}) async-start(), calls=%async_computation.2 | async-start | bytes 2621440 | tf_op jit(solution)/shard_map/reduce_scatter | solution.py:89
Sparse Core Ops, SparseCore 0:
  150.0 52.5 all-gather.1
  212.6 32.3 reduce-scatter.1
where the time goes:
time: 253 us; the launch traced here: 252 us
  waiting for transfers between devices  172 us (68%)
  starting transfers between devices  34 us (13%)
  matrix products  17.7 us (7%)
  between operations  14.2 us (6%)
  other arithmetic  8.98 us (4%)
  local copies, waits for them, and re-layouts  4.6 us (2%)
    ppermute x16, waiting for transfers between devices, from_behind(): lax.ppermute(value, axis, [(source, source + steps) for source in range(f...  87.5 us
    all_gather x1, waiting for transfers between devices, on_device(): lax.all_gather(x_grad, 'col', axis=1, tiled=True)  52.7 us
    ppermute x16, starting transfers between devices, from_behind(): lax.ppermute(value, axis, [(source, source + steps) for source in range(f...  34 us
    reduce_scatter x1, waiting for transfers between devices, on_device(): lax.psum_scatter(partial_grad.astype(jnp.bfloat16), 'row', scatter_dimens...  31.6 us
    dot_general x1, matrix products, on_device(): lax.dot_general(lax.all_gather(x_grad, 'col', axis=1, tiled=True), proj_w...  9.85 us
  transfers between devices with their start and end apart: 18, of which 18 were waited for; matrix products, arithmetic and copies ran while one was open for 0% of the time, Pallas kernels for 0%

commit v1 on v0

--- a/solution.py
+++ b/solution.py
@@ -80,8 +80,17 @@
     for tap in range(KW):
         accum = accum + conv_weight[tap][None, :] * extended[tap : tap + tokens_dev]
     x_grad = accum.astype(jnp.bfloat16)
+    mark_axis_part = lambda u_in, bus_axis, dim_no: jnp.concatenate(
+        lax.all_to_all(
+            jnp.stack([u_in for _ in range(lax.psum(1, bus_axis))], 0),
+            bus_axis,
+            split_axis=0,
+            concat_axis=0,
+        ),
+        dim_no,
+    )
     partial_grad = lax.dot_general(
-        lax.all_gather(x_grad, "col", axis=1, tiled=True),
+        mark_axis_part(x_grad, "col", 1),
         proj_weight,
         (((1,), (1,)), ((), ())),
         preferred_element_type=jnp.float32,

time: 253 us -> 244 us (0.964)
  waiting for transfers between devices: 172 us -> 135 us
  blocking collectives: 0 us -> 29.3 us
    all_gather x1 -> x0, waiting for transfers between devices: 52.7 us -> none  [on_device(): lax.all_gather(x_grad, 'col', axis=1, tiled=True)]
    all_to_all x0 -> x1, blocking collectives: none -> 29.3 us  [on_device(): lax.all_to_all(jnp.stack([u_in for _ in range(lax.psum(1, bus_axis))], 0)...]
    reduce_scatter x1, waiting for transfers between devices: 31.6 us -> 47.7 us  [on_device(): lax.psum_scatter(partial_grad.astype(jnp.bfloat16), 'row', scatter_dimens...]
  transfers between devices with their start and end apart: 18 -> 17, of which waited for: 18 -> 17; matrix products, arithmetic and copies ran while one was open for 0% -> 0% of each run, Pallas kernels for 0% -> 0%
where the time goes in v1:
time: 244 us
  waiting for transfers between devices  135 us (55%)
  starting transfers between devices  34 us (14%)
  blocking collectives  29.3 us (12%)
  matrix products  17.2 us (7%)
  between operations  14.2 us (6%)
  other arithmetic  8.18 us (3%)
  local copies, waits for them, and re-layouts  4.98 us (2%)
    ppermute x16, waiting for transfers between devices, from_behind(): lax.ppermute(value, axis, [(source, source + steps) for source in range(f...  87.5 us
    reduce_scatter x1, waiting for transfers between devices, on_device(): lax.psum_scatter(partial_grad.astype(jnp.bfloat16), 'row', scatter_dimens...  47.7 us
    ppermute x16, starting transfers between devices, from_behind(): lax.ppermute(value, axis, [(source, source + steps) for source in range(f...  34 us
    all_to_all x1, blocking collectives, on_device(): lax.all_to_all(jnp.stack([u_in for _ in range(lax.psum(1, bus_axis))], 0)...  29.3 us
    dot_general x1, matrix products, on_device(): lax.dot_general(mark_axis_part(x_grad, 'col', 1), proj_weight, (((1,), (1...  9.34 us
  transfers between devices with their start and end apart: 17, of which 17 were waited for; matrix products, arithmetic and copies ran while one was open for 0% of the time, Pallas kernels for 0%

profile of v1, /device:TPU:1, one launch (start us, length us, event | category | flops | bytes accessed | tf_op | source)
XLA Modules:
  0.0 243.6 jit_solution(11539175523707514088)
XLA Ops:
  7.2 2.3 reduce-window.6
  10.1 1.3 copy.27
  11.5 2.6 %constant_dynamic-slice_fusion = (bf16[512,1,256]{2,1,0:T(2,128)(2,1)S(1)}, bf16[512,1,256]{2,1,0:T(2,128)(2,1)S(1)}) fusion(bf16[512,4,256]{2,1,0:T(4,128)(2,1)} %param.15, s32[]{:T(128)S(6)} %select_n.30, bf16[512,4,256]{2,1,0:T(4,128)(2,1)} %param.14), kind=kLoop, calls=%fused_computation.48 | loop fusion | bytes 1048580 | tf_op jit(solution)/shard_map/jit(dynamic_index_in_dim)/dynamic_slice | solution.py:34
  14.1 0.3 fusion.17
  14.5 1.3 fusion.20
  15.8 4.3 %fusion.2 = f32[512,8,64]{0,2,1:T(8,128)} fusion(bf16[512,8,64]{0,2,1:T(8,128)(2,1)S(1)} %bitcast.44, f32[512,512]{1,0:T(8,128)} %fusion.20, f32[8,512]{1,0:T(8,128)S(1)} %get-tuple-element.49, pred[512,512]{1,0:T(8,128)(4,1)S(1)} %iota_compare_fusion), kind=kOutput, calls=%fused_computation.6 | convolution fusion | flops 276824064 | bytes 2899968 | tf_op jit(solution)/shard_map/hts,shd->thd/dot_general | solution.py:65
  20.1 119.6 %while.10 = (s32[]{:T(128)}, f32[8,64,256]{2,1,0:T(8,128)S(1)}, pred[]{:T(512)}, f32[8]{0:T(128)S(1)}, f32[8,64,256]{2,1,0:T(8,128)S(1)}, /*index=5*/f32[8,64,256]{2,1,0:T(8,128)S(1)}, s32[]{:T(128)}) while((s32[]{:T(128)}, f32[8,64,256]{2,1,0:T(8,128)S(1)}, pred[]{:T(512)}, f32[8]{0:T(128)S(1)}, f32[8,64,256]{2,1,0:T(8,128)S(1)}, ...), condition=%wide.region_3.4_spmd, body=%wide.region_2.3_spmd.sunk | while | flops 655362 | bytes 3670166 | solution.py:51
  20.2 5.2 %collective-permute-start = (bf16[8,64,256]{2,1,0:T(8,128)(2,1)S(1)}, bf16[8,64,256]{2,1,0:T(8,128)(2,1)S(1)}, u32[]{:S(2)}, u32[]{:S(2)}) collective-permute-start(bf16[8,64,256]{2,1,0:T(8,128)(2,1)S(1)} %add_convert_fusion.2), channel_id=1, source_target_pairs={{16,0},{32,16},{48,32},{64,48},{80,64},{96,80},{112,96},{128,112},... | collective-permute-start | bytes 786440 | tf_op jit(solution)/shard_map/while/body/eval_jaxpr/ppermute | solution.py:14
  25.4 3.8 %collective-permute-done = bf16[8,64,256]{2,1,0:T(8,128)(2,1)S(1)} collective-permute-done((bf16[8,64,256]{2,1,0:T(8,128)(2,1)S(1)}, bf16[8,64,256]{2,1,0:T(8,128)(2,1)S(1)}, u32[]{:S(2)}, u32[]{:S(2)}) %collective-permute-start) | collective-permute-done | bytes 262176 | tf_op jit(solution)/shard_map/while/body/eval_jaxpr/ppermute | solution.py:14
  29.4 1.9 collective-permute-start
  31.3 5.8 %collective-permute-done = bf16[8,64,256]{2,1,0:T(8,128)(2,1)S(1)} collective-permute-done((bf16[8,64,256]{2,1,0:T(8,128)(2,1)S(1)}, bf16[8,64,256]{2,1,0:T(8,128)(2,1)S(1)}, u32[]{:S(2)}, u32[]{:S(2)}) %collective-permute-start) | collective-permute-done | bytes 262176 | tf_op jit(solution)/shard_map/while/body/eval_jaxpr/ppermute | solution.py:14
  37.3 1.9 collective-permute-start
  39.2 5.8 %collective-permute-done = bf16[8,64,256]{2,1,0:T(8,128)(2,1)S(1)} collective-permute-done((bf16[8,64,256]{2,1,0:T(8,128)(2,1)S(1)}, bf16[8,64,256]{2,1,0:T(8,128)(2,1)S(1)}, u32[]{:S(2)}, u32[]{:S(2)}) %collective-permute-start) | collective-permute-done | bytes 262176 | tf_op jit(solution)/shard_map/while/body/eval_jaxpr/ppermute | solution.py:14
  45.2 1.9 collective-permute-start
  47.1 5.8 %collective-permute-done = bf16[8,64,256]{2,1,0:T(8,128)(2,1)S(1)} collective-permute-done((bf16[8,64,256]{2,1,0:T(8,128)(2,1)S(1)}, bf16[8,64,256]{2,1,0:T(8,128)(2,1)S(1)}, u32[]{:S(2)}, u32[]{:S(2)}) %collective-permute-start) | collective-permute-done | bytes 262176 | tf_op jit(solution)/shard_map/while/body/eval_jaxpr/ppermute | solution.py:14
  53.1 1.9 collective-permute-start
  55.0 5.8 %collective-permute-done = bf16[8,64,256]{2,1,0:T(8,128)(2,1)S(1)} collective-permute-done((bf16[8,64,256]{2,1,0:T(8,128)(2,1)S(1)}, bf16[8,64,256]{2,1,0:T(8,128)(2,1)S(1)}, u32[]{:S(2)}, u32[]{:S(2)}) %collective-permute-start) | collective-permute-done | bytes 262176 | tf_op jit(solution)/shard_map/while/body/eval_jaxpr/ppermute | solution.py:14
  61.0 1.9 collective-permute-start
  62.9 5.8 %collective-permute-done = bf16[8,64,256]{2,1,0:T(8,128)(2,1)S(1)} collective-permute-done((bf16[8,64,256]{2,1,0:T(8,128)(2,1)S(1)}, bf16[8,64,256]{2,1,0:T(8,128)(2,1)S(1)}, u32[]{:S(2)}, u32[]{:S(2)}) %collective-permute-start) | collective-permute-done | bytes 262176 | tf_op jit(solution)/shard_map/while/body/eval_jaxpr/ppermute | solution.py:14
  68.8 1.9 collective-permute-start
  70.8 5.8 %collective-permute-done = bf16[8,64,256]{2,1,0:T(8,128)(2,1)S(1)} collective-permute-done((bf16[8,64,256]{2,1,0:T(8,128)(2,1)S(1)}, bf16[8,64,256]{2,1,0:T(8,128)(2,1)S(1)}, u32[]{:S(2)}, u32[]{:S(2)}) %collective-permute-start) | collective-permute-done | bytes 262176 | tf_op jit(solution)/shard_map/while/body/eval_jaxpr/ppermute | solution.py:14
  76.7 1.9 collective-permute-start
  78.7 5.8 %collective-permute-done = bf16[8,64,256]{2,1,0:T(8,128)(2,1)S(1)} collective-permute-done((bf16[8,64,256]{2,1,0:T(8,128)(2,1)S(1)}, bf16[8,64,256]{2,1,0:T(8,128)(2,1)S(1)}, u32[]{:S(2)}, u32[]{:S(2)}) %collective-permute-start) | collective-permute-done | bytes 262176 | tf_op jit(solution)/shard_map/while/body/eval_jaxpr/ppermute | solution.py:14
  84.6 1.9 collective-permute-start
  86.5 5.8 %collective-permute-done = bf16[8,64,256]{2,1,0:T(8,128)(2,1)S(1)} collective-permute-done((bf16[8,64,256]{2,1,0:T(8,128)(2,1)S(1)}, bf16[8,64,256]{2,1,0:T(8,128)(2,1)S(1)}, u32[]{:S(2)}, u32[]{:S(2)}) %collective-permute-start) | collective-permute-done | bytes 262176 | tf_op jit(solution)/shard_map/while/body/eval_jaxpr/ppermute | solution.py:14
  92.5 1.9 collective-permute-start
  94.4 5.8 %collective-permute-done = bf16[8,64,256]{2,1,0:T(8,128)(2,1)S(1)} collective-permute-done((bf16[8,64,256]{2,1,0:T(8,128)(2,1)S(1)}, bf16[8,64,256]{2,1,0:T(8,128)(2,1)S(1)}, u32[]{:S(2)}, u32[]{:S(2)}) %collective-permute-start) | collective-permute-done | bytes 262176 | tf_op jit(solution)/shard_map/while/body/eval_jaxpr/ppermute | solution.py:14
  100.4 1.9 collective-permute-start
  102.3 5.8 %collective-permute-done = bf16[8,64,256]{2,1,0:T(8,128)(2,1)S(1)} collective-permute-done((bf16[8,64,256]{2,1,0:T(8,128)(2,1)S(1)}, bf16[8,64,256]{2,1,0:T(8,128)(2,1)S(1)}, u32[]{:S(2)}, u32[]{:S(2)}) %collective-permute-start) | collective-permute-done | bytes 262176 | tf_op jit(solution)/shard_map/while/body/eval_jaxpr/ppermute | solution.py:14
  108.3 1.9 collective-permute-start
  110.2 5.8 %collective-permute-done = bf16[8,64,256]{2,1,0:T(8,128)(2,1)S(1)} collective-permute-done((bf16[8,64,256]{2,1,0:T(8,128)(2,1)S(1)}, bf16[8,64,256]{2,1,0:T(8,128)(2,1)S(1)}, u32[]{:S(2)}, u32[]{:S(2)}) %collective-permute-start) | collective-permute-done | bytes 262176 | tf_op jit(solution)/shard_map/while/body/eval_jaxpr/ppermute | solution.py:14
  116.2 1.9 collective-permute-start
  118.1 5.8 %collective-permute-done = bf16[8,64,256]{2,1,0:T(8,128)(2,1)S(1)} collective-permute-done((bf16[8,64,256]{2,1,0:T(8,128)(2,1)S(1)}, bf16[8,64,256]{2,1,0:T(8,128)(2,1)S(1)}, u32[]{:S(2)}, u32[]{:S(2)}) %collective-permute-start) | collective-permute-done | bytes 262176 | tf_op jit(solution)/shard_map/while/body/eval_jaxpr/ppermute | solution.py:14
  124.1 1.9 collective-permute-start
  126.0 5.8 %collective-permute-done = bf16[8,64,256]{2,1,0:T(8,128)(2,1)S(1)} collective-permute-done((bf16[8,64,256]{2,1,0:T(8,128)(2,1)S(1)}, bf16[8,64,256]{2,1,0:T(8,128)(2,1)S(1)}, u32[]{:S(2)}, u32[]{:S(2)}) %collective-permute-start) | collective-permute-done | bytes 262176 | tf_op jit(solution)/shard_map/while/body/eval_jaxpr/ppermute | solution.py:14
  131.9 1.9 collective-permute-start
  133.9 5.8 %collective-permute-done = bf16[8,64,256]{2,1,0:T(8,128)(2,1)S(1)} collective-permute-done((bf16[8,64,256]{2,1,0:T(8,128)(2,1)S(1)}, bf16[8,64,256]{2,1,0:T(8,128)(2,1)S(1)}, u32[]{:S(2)}, u32[]{:S(2)}) %collective-permute-start) | collective-permute-done | bytes 262176 | tf_op jit(solution)/shard_map/while/body/eval_jaxpr/ppermute | solution.py:14
  139.7 2.0 fusion.5
  141.7 0.3 copy.29
  142.0 1.4 fusion.11
  143.5 1.9 collective-permute-start.1
  145.5 3.0 %collective-permute-done.1 = bf16[3,512]{1,0:T(4,128)(2,1)S(1)} collective-permute-done((bf16[3,512]{1,0:T(4,128)(2,1)S(1)}, bf16[3,512]{1,0:T(4,128)(2,1)S(1)}, u32[]{:S(2)}, u32[]{:S(2)}) %collective-permute-start.1) | collective-permute-done | bytes 3104 | tf_op jit(solution)/shard_map/ppermute | solution.py:14
  148.6 0.5 fusion.13
  149.1 0.2 copy.30
  149.4 29.3 %all_to_all.5 = bf16[4,512,512]{1,2,0:T(8,128)(2,1)S(1)} all-to-all(bf16[4,512,512]{1,2,0:T(8,128)(2,1)S(1)} %stack.2), channel_id=1, replica_groups=mesh['ctx'=16,'row'=4,'col'=4] {'col'}, dimensions={0} | all-to-all | bytes 4194304 | tf_op jit(solution)/shard_map/all_to_all | solution.py:84
  178.7 9.3 %convolution_convert_fusion = bf16[512,2048]{1,0:T(8,128)(2,1)} fusion(bf16[512,2048]{0,1:T(8,128)(2,1)S(1)} %bitcast.47, bf16[2048,2048]{1,0:T(8,128)(2,1)} %param.21), kind=kOutput, calls=%fused_computation.5 | convolution fusion | flops 4296015872 | bytes 12582912 | tf_op jit(solution)/shard_map/dot_general | solution.py:92
  188.1 0.9 add_bitcast_fusion
  189.0 47.7 %reduce-scatter.2.cloned.1.call-done = bf16[512,512]{1,0:T(8,128)(2,1)} async-done(((bf16[512,2048]{1,0:T(8,128)(2,1)}), bf16[512,512]{1,0:T(8,128)(2,1)}) %reduce-scatter.2.cloned.1.call-update) | async-done | bytes 524304 | tf_op jit(solution)/shard_map/reduce_scatter | solution.py:98
  (56 shorter events, 3.7 us)
Async XLA Ops:
  7.2 8.6 %copy-start = (f32[8,64,256]{2,1,0:T(8,128)S(1)}, f32[8,64,256]{2,1,0:T(8,128)}, u32[]{:S(2)}) copy-start(f32[8,64,256]{2,1,0:T(8,128)} %param.20) | copy-start | bytes 1572868
  7.2 229.6 %reduce-scatter.2.cloned.1.call-start = ((), (), s32[]{:S(2)}) async-start(), calls=%async_computation.2 | async-start | bytes 2621440 | tf_op jit(solution)/shard_map/reduce_scatter | solution.py:98
  20.1 119.6 %copy-start.2 = (f32[8,512]{1,0:T(8,128)S(1)}, f32[8,512]{1,0:T(8,128)}, u32[]{:S(2)}) copy-start(f32[8,512]{1,0:T(8,128)} %param.16) | copy-start | bytes 49156
  20.1 119.6 %copy-start.4 = (f32[8]{0:T(128)S(1)}, f32[8]{0:T(128)}, u32[]{:S(2)}) copy-start(f32[8]{0:T(128)} %param.18) | copy-start | bytes 100
  20.2 9.0 %collective-permute-start = (bf16[8,64,256]{2,1,0:T(8,128)(2,1)S(1)}, bf16[8,64,256]{2,1,0:T(8,128)(2,1)S(1)}, u32[]{:S(2)}, u32[]{:S(2)}) collective-permute-start(bf16[8,64,256]{2,1,0:T(8,128)(2,1)S(1)} %add_convert_fusion.2), channel_id=1, source_target_pairs={{16,0},{32,16},{48,32},{64,48},{80,64},{96,80},{112,96},{128,112},... | collective-permute-start | bytes 786440 | tf_op jit(solution)/shard_map/while/body/eval_jaxpr/ppermute | solution.py:14
  29.4 7.7 %collective-permute-start = (bf16[8,64,256]{2,1,0:T(8,128)(2,1)S(1)}, bf16[8,64,256]{2,1,0:T(8,128)(2,1)S(1)}, u32[]{:S(2)}, u32[]{:S(2)}) collective-permute-start(bf16[8,64,256]{2,1,0:T(8,128)(2,1)S(1)} %add_convert_fusion.2), channel_id=1, source_target_pairs={{16,0},{32,16},{48,32},{64,48},{80,64},{96,80},{112,96},{128,112},... | collective-permute-start | bytes 786440 | tf_op jit(solution)/shard_map/while/body/eval_jaxpr/ppermute | solution.py:14
  37.3 7.7 %collective-permute-start = (bf16[8,64,256]{2,1,0:T(8,128)(2,1)S(1)}, bf16[8,64,256]{2,1,0:T(8,128)(2,1)S(1)}, u32[]{:S(2)}, u32[]{:S(2)}) collective-permute-start(bf16[8,64,256]{2,1,0:T(8,128)(2,1)S(1)} %add_convert_fusion.2), channel_id=1, source_target_pairs={{16,0},{32,16},{48,32},{64,48},{80,64},{96,80},{112,96},{128,112},... | collective-permute-start | bytes 786440 | tf_op jit(solution)/shard_map/while/body/eval_jaxpr/ppermute | solution.py:14
  45.2 7.7 %collective-permute-start = (bf16[8,64,256]{2,1,0:T(8,128)(2,1)S(1)}, bf16[8,64,256]{2,1,0:T(8,128)(2,1)S(1)}, u32[]{:S(2)}, u32[]{:S(2)}) collective-permute-start(bf16[8,64,256]{2,1,0:T(8,128)(2,1)S(1)} %add_convert_fusion.2), channel_id=1, source_target_pairs={{16,0},{32,16},{48,32},{64,48},{80,64},{96,80},{112,96},{128,112},... | collective-permute-start | bytes 786440 | tf_op jit(solution)/shard_map/while/body/eval_jaxpr/ppermute | solution.py:14
  53.1 7.7 %collective-permute-start = (bf16[8,64,256]{2,1,0:T(8,128)(2,1)S(1)}, bf16[8,64,256]{2,1,0:T(8,128)(2,1)S(1)}, u32[]{:S(2)}, u32[]{:S(2)}) collective-permute-start(bf16[8,64,256]{2,1,0:T(8,128)(2,1)S(1)} %add_convert_fusion.2), channel_id=1, source_target_pairs={{16,0},{32,16},{48,32},{64,48},{80,64},{96,80},{112,96},{128,112},... | collective-permute-start | bytes 786440 | tf_op jit(solution)/shard_map/while/body/eval_jaxpr/ppermute | solution.py:14
  61.0 7.7 %collective-permute-start = (bf16[8,64,256]{2,1,0:T(8,128)(2,1)S(1)}, bf16[8,64,256]{2,1,0:T(8,128)(2,1)S(1)}, u32[]{:S(2)}, u32[]{:S(2)}) collective-permute-start(bf16[8,64,256]{2,1,0:T(8,128)(2,1)S(1)} %add_convert_fusion.2), channel_id=1, source_target_pairs={{16,0},{32,16},{48,32},{64,48},{80,64},{96,80},{112,96},{128,112},... | collective-permute-start | bytes 786440 | tf_op jit(solution)/shard_map/while/body/eval_jaxpr/ppermute | solution.py:14
  68.8 7.7 %collective-permute-start = (bf16[8,64,256]{2,1,0:T(8,128)(2,1)S(1)}, bf16[8,64,256]{2,1,0:T(8,128)(2,1)S(1)}, u32[]{:S(2)}, u32[]{:S(2)}) collective-permute-start(bf16[8,64,256]{2,1,0:T(8,128)(2,1)S(1)} %add_convert_fusion.2), channel_id=1, source_target_pairs={{16,0},{32,16},{48,32},{64,48},{80,64},{96,80},{112,96},{128,112},... | collective-permute-start | bytes 786440 | tf_op jit(solution)/shard_map/while/body/eval_jaxpr/ppermute | solution.py:14
  76.7 7.7 %collective-permute-start = (bf16[8,64,256]{2,1,0:T(8,128)(2,1)S(1)}, bf16[8,64,256]{2,1,0:T(8,128)(2,1)S(1)}, u32[]{:S(2)}, u32[]{:S(2)}) collective-permute-start(bf16[8,64,256]{2,1,0:T(8,128)(2,1)S(1)} %add_convert_fusion.2), channel_id=1, source_target_pairs={{16,0},{32,16},{48,32},{64,48},{80,64},{96,80},{112,96},{128,112},... | collective-permute-start | bytes 786440 | tf_op jit(solution)/shard_map/while/body/eval_jaxpr/ppermute | solution.py:14
  84.6 7.7 %collective-permute-start = (bf16[8,64,256]{2,1,0:T(8,128)(2,1)S(1)}, bf16[8,64,256]{2,1,0:T(8,128)(2,1)S(1)}, u32[]{:S(2)}, u32[]{:S(2)}) collective-permute-start(bf16[8,64,256]{2,1,0:T(8,128)(2,1)S(1)} %add_convert_fusion.2), channel_id=1, source_target_pairs={{16,0},{32,16},{48,32},{64,48},{80,64},{96,80},{112,96},{128,112},... | collective-permute-start | bytes 786440 | tf_op jit(solution)/shard_map/while/body/eval_jaxpr/ppermute | solution.py:14
  92.5 7.7 %collective-permute-start = (bf16[8,64,256]{2,1,0:T(8,128)(2,1)S(1)}, bf16[8,64,256]{2,1,0:T(8,128)(2,1)S(1)}, u32[]{:S(2)}, u32[]{:S(2)}) collective-permute-start(bf16[8,64,256]{2,1,0:T(8,128)(2,1)S(1)} %add_convert_fusion.2), channel_id=1, source_target_pairs={{16,0},{32,16},{48,32},{64,48},{80,64},{96,80},{112,96},{128,112},... | collective-permute-start | bytes 786440 | tf_op jit(solution)/shard_map/while/body/eval_jaxpr/ppermute | solution.py:14
  100.4 7.7 %collective-permute-start = (bf16[8,64,256]{2,1,0:T(8,128)(2,1)S(1)}, bf16[8,64,256]{2,1,0:T(8,128)(2,1)S(1)}, u32[]{:S(2)}, u32[]{:S(2)}) collective-permute-start(bf16[8,64,256]{2,1,0:T(8,128)(2,1)S(1)} %add_convert_fusion.2), channel_id=1, source_target_pairs={{16,0},{32,16},{48,32},{64,48},{80,64},{96,80},{112,96},{128,112},... | collective-permute-start | bytes 786440 | tf_op jit(solution)/shard_map/while/body/eval_jaxpr/ppermute | solution.py:14
  108.3 7.7 %collective-permute-start = (bf16[8,64,256]{2,1,0:T(8,128)(2,1)S(1)}, bf16[8,64,256]{2,1,0:T(8,128)(2,1)S(1)}, u32[]{:S(2)}, u32[]{:S(2)}) collective-permute-start(bf16[8,64,256]{2,1,0:T(8,128)(2,1)S(1)} %add_convert_fusion.2), channel_id=1, source_target_pairs={{16,0},{32,16},{48,32},{64,48},{80,64},{96,80},{112,96},{128,112},... | collective-permute-start | bytes 786440 | tf_op jit(solution)/shard_map/while/body/eval_jaxpr/ppermute | solution.py:14
  116.2 7.7 %collective-permute-start = (bf16[8,64,256]{2,1,0:T(8,128)(2,1)S(1)}, bf16[8,64,256]{2,1,0:T(8,128)(2,1)S(1)}, u32[]{:S(2)}, u32[]{:S(2)}) collective-permute-start(bf16[8,64,256]{2,1,0:T(8,128)(2,1)S(1)} %add_convert_fusion.2), channel_id=1, source_target_pairs={{16,0},{32,16},{48,32},{64,48},{80,64},{96,80},{112,96},{128,112},... | collective-permute-start | bytes 786440 | tf_op jit(solution)/shard_map/while/body/eval_jaxpr/ppermute | solution.py:14
  124.1 7.7 %collective-permute-start = (bf16[8,64,256]{2,1,0:T(8,128)(2,1)S(1)}, bf16[8,64,256]{2,1,0:T(8,128)(2,1)S(1)}, u32[]{:S(2)}, u32[]{:S(2)}) collective-permute-start(bf16[8,64,256]{2,1,0:T(8,128)(2,1)S(1)} %add_convert_fusion.2), channel_id=1, source_target_pairs={{16,0},{32,16},{48,32},{64,48},{80,64},{96,80},{112,96},{128,112},... | collective-permute-start | bytes 786440 | tf_op jit(solution)/shard_map/while/body/eval_jaxpr/ppermute | solution.py:14
  131.9 7.7 %collective-permute-start = (bf16[8,64,256]{2,1,0:T(8,128)(2,1)S(1)}, bf16[8,64,256]{2,1,0:T(8,128)(2,1)S(1)}, u32[]{:S(2)}, u32[]{:S(2)}) collective-permute-start(bf16[8,64,256]{2,1,0:T(8,128)(2,1)S(1)} %add_convert_fusion.2), channel_id=1, source_target_pairs={{16,0},{32,16},{48,32},{64,48},{80,64},{96,80},{112,96},{128,112},... | collective-permute-start | bytes 786440 | tf_op jit(solution)/shard_map/while/body/eval_jaxpr/ppermute | solution.py:14
  139.7 5.7 %copy-start.3 = (f32[4,512]{1,0:T(4,128)S(1)}, f32[4,512]{1,0:T(4,128)}, u32[]{:S(2)}) copy-start(f32[4,512]{1,0:T(4,128)} %param.19) | copy-start | bytes 24580
  143.5 4.9 %collective-permute-start.1 = (bf16[3,512]{1,0:T(4,128)(2,1)S(1)}, bf16[3,512]{1,0:T(4,128)(2,1)S(1)}, u32[]{:S(2)}, u32[]{:S(2)}) collective-permute-start(bf16[3,512]{1,0:T(4,128)(2,1)S(1)} %slice.50), channel_id=1, source_target_pairs={{16,0},{32,16},{48,32},{64,48},{80,64},{96,80},{112,96},{128,112},... | collective-permute-start | bytes 9224 | tf_op jit(solution)/shard_map/ppermute | solution.py:14
  149.0 39.0 %copy-start.1 = (bf16[512,512]{1,0:T(8,128)(2,1)}, bf16[512,512]{1,0:T(8,128)(2,1)S(1)}, u32[]{:S(2)}) copy-start(bf16[512,512]{1,0:T(8,128)(2,1)S(1)} %fusion.13) | copy-start | bytes 1572868
Sparse Core Ops, SparseCore 0:
  188.2 48.4 reduce-scatter.1
